TPU v7x, 256 devices: a whole 4x4x8 slice. The times are simulated.
256 devices in a mesh: rep: 16 (over y, z_lo), fsdp: 16 (over z_hi, x, core).
Axes of the slice: x: 4, y: 4, z: 8 (z_hi: 2, z_lo: 4; z = z_hi * 4 + z_lo), core: 2. Of those that a mesh axis runs over, the one named last changes fastest.
Arguments:
- hidden_in: bfloat16 [16, 16, 256, 4096], P('rep', 'fsdp'), may hold values from -6 to 6
- scan_in: bfloat16 [16, 16, 256, 4096], P('rep', 'fsdp'), may hold values from -6 to 6
- grad_out: bfloat16 [16, 16, 256, 4096], P('rep', 'fsdp'), may hold values from -6 to 6
- episodes: int32 [16, 16, 256], P('rep', 'fsdp'), may hold values from 0 to 2, never falling along the last dimension, each value on 1 to 128 neighbouring positions
- gossip_step: int32 [1], replicated, may hold values from 0 to 63
- state_proj: float32 [16, 4096, 256], P('rep', 'fsdp'), may hold values from -0.01953125 to 0.01953125
- step_proj: float32 [16, 32, 4096], P('rep', None, 'fsdp'), may hold values from -0.09375 to 0.09375
- decay_log: float32 [16, 32], P('rep'), may hold values from -5.5 to -3
- step_bias: float32 [16, 32], P('rep'), may hold values from -1 to 1
Outputs:
- layer_grad: bfloat16 [16, 16, 256, 4096], P('rep', 'fsdp')
- scan_grad: bfloat16 [16, 16, 256, 4096], P('rep', 'fsdp')
- new_state_proj: float32 [16, 4096, 256], P('rep', 'fsdp')
- new_step_proj: float32 [16, 32, 4096], P('rep', None, 'fsdp')
- new_decay_log: float32 [16, 32], P('rep')
- new_step_bias: float32 [16, 32], P('rep')
Inputs may be any that keep to these rules, and one draw needn't show every extreme that they name: `episodes`: within each sequence the episode ids never fall; an episode has at most half of 256 tokens, and one has exactly that many.
All inputs are finite; a program needn't handle non-finite values.
Results may differ from a plain program's by a relative error of at most 0.0058.
The roundings to bfloat16 on the way count: a program that leaves them out, or rounds other values in their place, can miss the bound.
Values may be sent and summed in bfloat16 or wider, within the bound.
A program may use at most 128 MiB of HBM per device.

v0:
```python
import functools

import jax
import jax.numpy as jnp
from jax import lax
from jax.experimental import pallas as pl
from jax.experimental.pallas import tpu as pltpu
from jax.sharding import PartitionSpec as P

MESH = pl.DeviceIdType.MESH
F32 = jnp.float32
BF16 = jnp.bfloat16
HIGH = lax.Precision.HIGHEST
LOG2E = 1.4426950408889634
TINY = 1e-37
CAP = 60.0
RATE = 0.1
EPS = 1e-6
WIDTH = 128


def nn(a, b, precision=None):
    return lax.dot_general(
        a, b, (((1,), (0,)), ((), ())), precision=precision, preferred_element_type=F32
    )


def nt(a, b, precision=None):
    return lax.dot_general(
        a, b, (((1,), (1,)), ((), ())), precision=precision, preferred_element_type=F32
    )


def split3(value):
    high = value.astype(BF16).astype(F32)
    rest = value - high
    mid = rest.astype(BF16).astype(F32)
    return high, mid, rest - mid


def layer_kernel(
    dims,
    bit_ref,
    own_ref,
    state_ref,
    step_ref,
    hid_hbm,
    val_hbm,
    cot_hbm,
    epc_ref,
    epr_ref,
    acol_ref,
    bcol_ref,
    head_ref,
    lay_hbm,
    sgr_hbm,
    nstate_ref,
    nstep_ref,
    nhead_ref,
    hid,
    val,
    cot,
    wts,
    dwo,
    acc,
    from_core,
    hop1,
    hop2,
    from_z,
    part_p,
    part_g,
    part_s,
    zsend,
    gsend,
    heads_in,
    sums_in,
    final_send,
    lay,
    sgr,
    feat,
    du3,
    rhs,
    scores,
    ds0,
    ds1,
    mrow,
    mcol,
    fgt,
    fg,
    fgl,
    local_sem,
    ssem,
    rsem,
):
    heads, reps, seqs, chunk, rows = dims
    half = rows // 2
    bits = reps.bit_length() - 1
    state2 = 2 * WIDTH
    me = lax.axis_index("fsdp")
    rep = lax.axis_index("rep")
    core = lax.rem(me, 2)
    x_at = lax.rem(lax.div(me, 2), 4)
    z_at = lax.div(me, 8)

    def index_of(z, x, c):
        return z * 8 + lax.rem(x, 4) * 2 + c

    other_z = 1 - z_at
    other_c = 1 - core
    right = {"fsdp": index_of(z_at, x_at + 1, core)}
    left = {"fsdp": index_of(z_at, x_at + 3, core)}
    across = {"fsdp": index_of(other_z, x_at, core)}
    twin = {"fsdp": index_of(z_at, x_at, other_c)}
    peers = [{"fsdp": lax.rem(me + k, seqs)} for k in range(1, seqs)]
    mates = []
    for bit in range(bits):
        gap = 1 << bit
        mates.append({"rep": rep + gap * (1 - 2 * lax.rem(lax.div(rep, gap), 2))})

    used = [0]

    def remote(src, dst, number, device):
        return pltpu.make_async_remote_copy(
            src_ref=src,
            dst_ref=dst,
            send_sem=ssem.at[number],
            recv_sem=rsem.at[number],
            device_id=device,
            device_id_type=MESH,
        )

    started = []

    def send(src, dst, device):
        number = used[0]
        used[0] += 1
        copy = remote(src, dst, number, device)
        copy.start()
        started.append(copy)
        return number

    def landed(dst, number):
        remote(dst, dst, number, twin).wait_recv()

    loads = [
        pltpu.make_async_copy(hid_hbm, hid, local_sem.at[0]),
        pltpu.make_async_copy(val_hbm, val, local_sem.at[1]),
        pltpu.make_async_copy(cot_hbm, cot, local_sem.at[2]),
        pltpu.make_async_copy(own_ref, wts.at[me], local_sem.at[3]),
    ]
    for load in loads:
        load.start()

    barrier = pltpu.get_barrier_semaphore()
    for device in peers + mates:
        pl.semaphore_signal(barrier, inc=1, device_id=device, device_id_type=MESH)
    pl.semaphore_wait(barrier, len(peers) + len(mates))

    top = pl.ds(0, half)
    low = pl.ds(half, half)
    mine = wts.at[me]
    n_across = send(own_ref, mine, across)
    n_right = send(own_ref, mine, right)
    n_left = send(own_ref, mine, left)
    n_twin = [send(own_ref, mine, twin)]

    row_id = lax.broadcasted_iota(jnp.int32, (WIDTH, chunk), 0)

    def fill(h, carry):
        lane = ((row_id & (heads - 1)) == h) & (row_id < 3 * heads)
        rhs[h] = jnp.where(lane, 1.0, 0.0).astype(BF16)
        return carry

    lax.fori_loop(0, heads, fill, 0)

    def spread(z, n_r, n_l):
        at_l = index_of(z, x_at + 3, core)
        at_r = index_of(z, x_at + 1, core)
        landed(wts.at[at_l], n_r)
        f_r = send(wts.at[at_l, top], wts.at[at_l, top], right)
        n_twin.append(send(wts.at[at_l], wts.at[at_l], twin))
        landed(wts.at[at_r], n_l)
        f_l = send(wts.at[at_r, low], wts.at[at_r, low], left)
        n_twin.append(send(wts.at[at_r], wts.at[at_r], twin))
        return f_r, f_l

    def last(z, f_r, f_l):
        at_2 = index_of(z, x_at + 2, core)
        landed(wts.at[at_2, top], f_r)
        landed(wts.at[at_2, low], f_l)
        n_twin.append(send(wts.at[at_2], wts.at[at_2], twin))

    forward = spread(z_at, n_right, n_left)
    at_z = index_of(other_z, x_at, core)
    landed(wts.at[at_z], n_across)
    n_right2 = send(wts.at[at_z], wts.at[at_z], right)
    n_left2 = send(wts.at[at_z], wts.at[at_z], left)
    n_twin.append(send(wts.at[at_z], wts.at[at_z], twin))
    last(z_at, *forward)
    forward = spread(other_z, n_right2, n_left2)
    last(other_z, *forward)
    order = [
        (z_at, 0),
        (z_at, 3),
        (z_at, 1),
        (other_z, 0),
        (z_at, 2),
        (other_z, 3),
        (other_z, 1),
        (other_z, 2),
    ]
    for (z, dx), number in zip(order, n_twin):
        landed(wts.at[index_of(z, x_at + dx, other_c)], number)
    for load in loads:
        load.wait()

    n_part_p = [send(own_ref, part_p.at[bit], mates[bit]) for bit in range(bits)]

    feat[...] = jnp.zeros_like(feat)
    logits = jnp.zeros((heads, chunk), F32)
    for f in range(seqs):
        tokens = hid[:, f * chunk : (f + 1) * chunk]
        feat[...] += nn(tokens, wts[f, :state2, :])
        logits += nt(wts[f, state2:, :], tokens)
    logits = logits + bcol_ref[...]
    small = jnp.exp(-jnp.abs(logits))
    log_part = jnp.where(
        small < 0.01, small * (1.0 - small * (0.5 - small * (1.0 / 3.0))), jnp.log(1.0 + small)
    )
    step = jnp.maximum(logits, 0.0) + log_part
    gate = jnp.where(logits >= 0.0, 1.0, small) / (1.0 + small)
    step_safe = jnp.maximum(step, TINY)
    ratio = jnp.where(logits < -20.0, 1.0, gate / step_safe)
    decay = -jnp.exp(acol_ref[...])
    at_u = lax.broadcasted_iota(jnp.int32, (chunk, chunk), 0)
    at_t = lax.broadcasted_iota(jnp.int32, (chunk, chunk), 1)
    upper = jnp.where(at_u <= at_t, 1.0, 0.0)
    c2 = nn(decay * step, upper, HIGH) * LOG2E
    du = jnp.log2(step_safe) - c2
    parts = split3(du) + (jnp.ones((WIDTH - 3 * heads, chunk), F32),)
    du3[...] = jnp.concatenate(parts, axis=0).T.astype(BF16)
    c_parts = split3(c2)
    for k in range(3):
        rhs[:, 3 * heads + k, :] = c_parts[k].astype(BF16)
    b_proj = feat[:, :WIDTH]
    c_proj = feat[:, WIDTH:]
    allowed = (at_u <= at_t) & (epc_ref[...] == epr_ref[...])
    scores[...] = jnp.where(allowed, nt(b_proj, c_proj, HIGH), 0.0)
    ds0[...] = jnp.zeros_like(ds0)
    ds1[...] = jnp.zeros_like(ds1)
    ones8 = jnp.ones((8, WIDTH), BF16)

    def head_step(h, carry):
        lanes = pl.ds(pl.multiple_of(h * WIDTH, WIDTH), WIDTH)
        xh = val[:, lanes]
        gh = cot[:, lanes]
        rh = rhs[h]
        g0 = nt(xh[:WIDTH], gh)
        g1 = nt(xh[WIDTH:], gh[WIDTH:])
        e0 = jnp.exp2(jnp.minimum(nn(du3[:WIDTH], rh), CAP))
        e1 = jnp.exp2(jnp.minimum(nn(du3[WIDTH:], rh[:, WIDTH:]), CAP))
        ds0[...] += g0 * e0
        ds1[...] += g1 * e1
        v0 = e0 * scores[:WIDTH]
        v1 = e1 * scores[WIDTH:, WIDTH:]
        m0 = jnp.sum((v0 * g0).reshape(WIDTH // 8, 8, -1), axis=0)
        m1 = jnp.sum((v1 * g1).reshape(WIDTH // 8, 8, -1), axis=0)
        mrow[h, :, :WIDTH] = m0[:, :WIDTH]
        mrow[h, :, WIDTH:] = m0[:, WIDTH:] + m1
        dx0 = nn(v0.astype(BF16), gh)
        dx1 = nn(v1.astype(BF16), gh[WIDTH:])
        dx = jnp.concatenate([dx0, dx1], axis=0)
        sgr[:, lanes] = dx.astype(BF16)
        prod = dx * xh.astype(F32)
        high = prod.astype(BF16)
        rest = (prod - high.astype(F32)).astype(BF16)
        col = nt(ones8, high) + nt(ones8, rest)
        mcol[h] = col
        return carry

    lax.fori_loop(0, heads, head_step, 0)
    out_sgr = pltpu.make_async_copy(sgr, sgr_hbm, local_sem.at[4])
    out_sgr.start()

    lower = jnp.where(at_u >= at_t, 1.0, 0.0)
    mc = jnp.sum(mcol[...], axis=1) * 0.125
    drate = nn(jnp.sum(mrow[...], axis=1) - mc, lower, HIGH)
    dlogit = mc * ratio + gate * (decay * drate)
    ddecay = decay * step * drate
    stack = jnp.concatenate(
        [ddecay, dlogit, jnp.zeros((WIDTH - 2 * heads, chunk), F32)], axis=0
    )
    heads_in[me] = nt(jnp.ones((8, chunk), F32), stack, HIGH)
    ds_full = jnp.concatenate(
        [
            ds0[...],
            jnp.concatenate([jnp.zeros((WIDTH, WIDTH), F32), ds1[...]], axis=1),
        ],
        axis=0,
    )
    ds_full = jnp.where(allowed, ds_full, 0.0)
    db = nn(ds_full, c_proj, HIGH)
    dct = nn(b_proj.T, ds_full, HIGH)
    fgt[:WIDTH] = db.T.astype(BF16)
    fgt[WIDTH:state2] = dct.astype(BF16)
    fgt[state2:] = dlogit.astype(BF16)
    fg[:, :WIDTH] = db.astype(BF16)
    fg[:, WIDTH:] = dct.T.astype(BF16)
    wide = jnp.concatenate([dlogit, jnp.zeros((WIDTH - heads, chunk), F32)], axis=0)
    fgl[...] = wide.T.astype(BF16)

    n_heads = [send(heads_in.at[me], heads_in.at[me], device) for device in peers]

    places = [(z, dx) for z in (other_z, z_at) for dx in (2, 1, 3, 0)]

    def columns(index):
        return pl.ds(pl.multiple_of(index * chunk, chunk), chunk)

    n_core = []
    for slot, (z, dx) in enumerate(places):
        index = index_of(z, x_at + dx, other_c)
        dwo[slot] = nn(fgt[...], hid[:, columns(index)]).astype(BF16)
        n_core.append(send(dwo.at[slot], from_core.at[slot], twin))

    def own_part(slot):
        z, dx = places[slot]
        index = index_of(z, x_at + dx, core)
        total = nn(fgt[...], hid[:, columns(index)])
        landed(from_core.at[slot], n_core[slot])
        return total + from_core[slot].astype(F32)

    def layer_part(index):
        spot = columns(index)
        w = wts[index]
        lay[:, spot] = (
            nt(fg[...], w[:state2]) + nn(fgl[:, :heads], w[state2:])
        ).astype(BF16)

    def ring(base, k):
        two = own_part(base)
        acc[base] = two.astype(BF16)
        r1 = send(acc.at[base, top], hop1.at[k, 0], right)
        l1 = send(acc.at[base, low], hop1.at[k, 1], left)
        plus = own_part(base + 1)
        minus = own_part(base + 2)
        acc[base + 1, low] = plus[half:].astype(BF16)
        acc[base + 2, top] = minus[:half].astype(BF16)
        r2 = send(acc.at[base + 1, low], hop2.at[k, 0, low], right)
        l2 = send(acc.at[base + 2, top], hop2.at[k, 1, top], left)
        zero = own_part(base + 3)
        return r1, l1, r2, l2, plus[:half], minus[half:], zero

    def ring_next(base, k, r1, l1, plus, minus):
        landed(hop1.at[k, 0], r1)
        acc[base + 1, top] = (plus + hop1[k, 0].astype(F32)).astype(BF16)
        r3 = send(acc.at[base + 1, top], hop2.at[k, 0, top], right)
        landed(hop1.at[k, 1], l1)
        acc[base + 2, low] = (minus + hop1[k, 1].astype(F32)).astype(BF16)
        l3 = send(acc.at[base + 2, low], hop2.at[k, 1, low], left)
        return r3, l3

    def ring_end(k, r2, l2, r3, l3, zero):
        landed(hop2.at[k, 0, low], r2)
        landed(hop2.at[k, 1, top], l2)
        landed(hop2.at[k, 0, top], r3)
        landed(hop2.at[k, 1, low], l3)
        return zero + hop2[k, 0].astype(F32) + hop2[k, 1].astype(F32)

    r1, l1, r2, l2, plus, minus, zero = ring(0, 0)
    for index in range(0, 4):
        layer_part(index)
    r3, l3 = ring_next(0, 0, r1, l1, plus, minus)
    s1, m1, s2, m2, plus, minus, zero2 = ring(4, 1)
    for index in range(4, 8):
        layer_part(index)
    done = ring_end(0, r2, l2, r3, l3, zero)
    zsend[...] = done.astype(BF16)
    n_z = send(zsend, from_z, across)
    s3, m3 = ring_next(4, 1, s1, m1, plus, minus)
    for index in range(8, seqs):
        layer_part(index)
    out_lay = pltpu.make_async_copy(lay, lay_hbm, local_sem.at[5])
    out_lay.start()
    total = ring_end(1, s2, m2, s3, m3, zero2)
    landed(from_z, n_z)
    grad = total + from_z[...].astype(F32)
    gsend[...] = grad.astype(BF16)
    n_part_g = [send(gsend, part_g.at[bit], mates[bit]) for bit in range(bits)]

    def lanes_sum(value):
        total = jnp.sum(value * value, axis=0, keepdims=True)
        return total[:, :WIDTH] + total[:, WIDTH:]

    state_own = state_ref[...]
    step_own = step_ref[...]
    sums_in[me] = jnp.concatenate(
        [
            lanes_sum(grad[:state2]),
            lanes_sum(grad[state2:]),
            lanes_sum(state_own),
            lanes_sum(step_own),
            jnp.zeros((4, WIDTH), F32),
        ],
        axis=0,
    )
    n_sums = [send(sums_in.at[me], sums_in.at[me], device) for device in peers]

    for k, number in enumerate(n_heads):
        landed(heads_in.at[lax.rem(me + seqs - k - 1, seqs)], number)
    head_grad = jnp.sum(heads_in[...], axis=0)[:1]
    head_own = head_ref[...]
    head_sq = jnp.sum(head_own * head_own, axis=1, keepdims=True) / (2 * heads)
    hgrad_sq = jnp.sum(head_grad * head_grad, axis=1, keepdims=True) / (2 * heads)
    head_trust = jnp.sqrt(head_sq) / jnp.sqrt(hgrad_sq + EPS)
    head_new = head_own - RATE * head_trust * head_grad

    for k, number in enumerate(n_sums):
        landed(sums_in.at[lax.rem(me + seqs - k - 1, seqs)], number)
    squares = jnp.sum(jnp.sum(sums_in[...], axis=0), axis=1, keepdims=True)
    width = seqs * chunk
    state_trust = jnp.sqrt(squares[2:3] / (width * state2)) / jnp.sqrt(
        squares[0:1] / (width * state2) + EPS
    )
    step_trust = jnp.sqrt(squares[3:4] / (width * heads)) / jnp.sqrt(
        squares[1:2] / (width * heads) + EPS
    )
    final = jnp.concatenate(
        [
            head_new,
            jnp.broadcast_to(state_trust, (1, WIDTH)),
            jnp.broadcast_to(step_trust, (1, WIDTH)),
            jnp.zeros((5, WIDTH), F32),
        ],
        axis=0,
    )
    final_send[...] = final
    n_final = [send(final_send, part_s.at[bit], mates[bit]) for bit in range(bits)]
    for bit in range(bits):
        landed(part_p.at[bit], n_part_p[bit])
        landed(part_g.at[bit], n_part_g[bit])
        landed(part_s.at[bit], n_final[bit])
    bit = bit_ref[0]
    mate_p = part_p[bit].astype(F32)
    mate_g = part_g[bit].astype(F32)
    mate_s = part_s[bit]
    move = state_trust * grad[:state2] + mate_s[1:2, :1] * mate_g[:state2]
    nstate_ref[...] = 0.5 * (state_own + mate_p[:state2]) - (0.5 * RATE) * move.T
    move = step_trust * grad[state2:] + mate_s[2:3, :1] * mate_g[state2:]
    nstep_ref[...] = 0.5 * (step_own + mate_p[state2:]) - (0.5 * RATE) * move
    nhead_ref[...] = 0.5 * (final + mate_s)

    out_sgr.wait()
    out_lay.wait()
    for copy in started:
        copy.wait_send()


def count_copies(reps, seqs):
    bits = reps.bit_length() - 1
    return 4 + 2 * 4 + 3 + 2 + 3 * bits + 2 * (seqs - 1) + 8 + 12 + 1


def on_device(
    hidden_in, scan_in, grad_out, episodes, gossip_step, state_proj, step_proj, decay_log, step_bias
):
    reps = lax.axis_size("rep")
    seqs = lax.axis_size("fsdp")
    bits = reps.bit_length() - 1
    chosen = gossip_step % bits
    state_own = state_proj[0]
    step_own = step_proj[0]
    own = jnp.concatenate([state_own, step_own], axis=0).astype(BF16)
    heads = step_own.shape[0]
    length, inner = scan_in.shape[2:]
    model = hidden_in.shape[3]
    chunk = model // seqs
    rows = own.shape[0]
    state2 = 2 * WIDTH
    episode = episodes[0, 0]
    head_row = jnp.concatenate(
        [decay_log[0], step_bias[0], jnp.zeros((WIDTH - 2 * heads,), F32)]
    ).reshape(1, WIDTH)
    half = rows // 2
    vmem = pl.BlockSpec(memory_space=pltpu.VMEM)
    anyspace = pl.BlockSpec(memory_space=pl.ANY)
    copies = count_copies(reps, seqs) + 8
    outs = pl.pallas_call(
        functools.partial(layer_kernel, (heads, reps, seqs, chunk, rows)),
        out_shape=(
            jax.ShapeDtypeStruct((length, model), BF16),
            jax.ShapeDtypeStruct((length, inner), BF16),
            jax.ShapeDtypeStruct((chunk, state2), F32),
            jax.ShapeDtypeStruct((heads, chunk), F32),
            jax.ShapeDtypeStruct((8, WIDTH), F32),
        ),
        in_specs=[pl.BlockSpec(memory_space=pltpu.SMEM), vmem, vmem, vmem]
        + [anyspace] * 3
        + [vmem] * 5,
        out_specs=(anyspace, anyspace, vmem, vmem, vmem),
        scratch_shapes=[
            pltpu.VMEM((length, model), BF16),
            pltpu.VMEM((length, inner), BF16),
            pltpu.VMEM((length, inner), BF16),
            pltpu.VMEM((seqs, rows, chunk), BF16),
            pltpu.VMEM((8, rows, chunk), BF16),
            pltpu.VMEM((8, rows, chunk), BF16),
            pltpu.VMEM((8, rows, chunk), BF16),
            pltpu.VMEM((2, 2, half, chunk), BF16),
            pltpu.VMEM((2, 2, rows, chunk), BF16),
            pltpu.VMEM((rows, chunk), BF16),
            pltpu.VMEM((bits, rows, chunk), BF16),
            pltpu.VMEM((bits, rows, chunk), BF16),
            pltpu.VMEM((bits, 8, WIDTH), F32),
            pltpu.VMEM((rows, chunk), BF16),
            pltpu.VMEM((rows, chunk), BF16),
            pltpu.VMEM((seqs, 8, WIDTH), F32),
            pltpu.VMEM((seqs, 8, WIDTH), F32),
            pltpu.VMEM((8, WIDTH), F32),
            pltpu.VMEM((length, model), BF16),
            pltpu.VMEM((length, inner), BF16),
            pltpu.VMEM((length, state2), F32),
            pltpu.VMEM((length, WIDTH), BF16),
            pltpu.VMEM((heads, WIDTH, length), BF16),
            pltpu.VMEM((length, length), F32),
            pltpu.VMEM((WIDTH, length), F32),
            pltpu.VMEM((WIDTH, WIDTH), F32),
            pltpu.VMEM((heads, 8, length), F32),
            pltpu.VMEM((heads, 8, length), F32),
            pltpu.VMEM((rows, length), BF16),
            pltpu.VMEM((length, state2), BF16),
            pltpu.VMEM((length, WIDTH), BF16),
            pltpu.SemaphoreType.DMA((6,)),
            pltpu.SemaphoreType.DMA((copies,)),
            pltpu.SemaphoreType.DMA((copies,)),
        ],
        compiler_params=pltpu.CompilerParams(
            collective_id=0, has_side_effects=True, vmem_limit_bytes=60 * 1024 * 1024
        ),
    )(
        chosen.astype(jnp.int32),
        own,
        state_own,
        step_own,
        hidden_in[0, 0],
        scan_in[0, 0],
        grad_out[0, 0],
        episode[:, None],
        episode[None, :],
        decay_log[0][:, None],
        step_bias[0][:, None],
        head_row,
    )
    layer_grad, scan_grad, new_state, new_step, new_head = outs
    return (
        layer_grad[None, None],
        scan_grad[None, None],
        new_state[None],
        new_step[None],
        new_head[:1, :heads],
        new_head[:1, heads : 2 * heads],
    )


def solution(mesh):
    in_specs = (
        P("rep", "fsdp", None, None),
        P("rep", "fsdp", None, None),
        P("rep", "fsdp", None, None),
        P("rep", "fsdp", None),
        P(),
        P("rep", "fsdp", None),
        P("rep", None, "fsdp"),
        P("rep", None),
        P("rep", None),
    )
    out_specs = (
        P("rep", "fsdp", None, None),
        P("rep", "fsdp", None, None),
        P("rep", "fsdp", None),
        P("rep", None, "fsdp"),
        P("rep", None),
        P("rep", None),
    )
    return jax.shard_map(
        on_device, mesh=mesh, in_specs=in_specs, out_specs=out_specs, check_vma=False
    )
```

profile of v0, /device:TPU:1, one launch (start us, length us, event | category | flops | bytes accessed | tf_op | source)
XLA Modules:
  0.0 101.4 jit_solution(7500882379250288596)
XLA Ops:
  1.3 1.3 %maximum_bitcast_fusion.head_ref = f32[1,128]{1,0:T(1,128)} fusion(f32[64]{0:T(128)S(1)} %broadcast_in_dim.15, f32[32]{0:T(128)} %bitcast.30, f32[32]{0:T(128)} %bitcast.32), kind=kLoop, calls=%fused_computation.1 | loop fusion | flops 256 | bytes 1024 | tf_op jit(solution)/shard_map/reshape | solution.py:482
  2.6 1.3 %copy.19.bcol_ref = f32[32,1]{1,0:T(8,128)} copy(f32[32,1]{0,1:T(1,128)} %bitcast.31) | data formatting | bytes 256 | tf_op jit(solution)/shard_map/broadcast_in_dim;squeeze | solution.py:550
  3.9 1.3 %copy.18.acol_ref = f32[32,1]{1,0:T(8,128)} copy(f32[32,1]{0,1:T(1,128)} %bitcast.33) | data formatting | bytes 256 | tf_op jit(solution)/shard_map/broadcast_in_dim;squeeze | solution.py:549
  5.2 0.8 bitcast_convert_fusion
  6.0 1.5 %copy.17.epc_ref = s32[256,1]{1,0:T(8,128)} copy(s32[256,1]{0,1:T(1,128)} %bitcast.28) | data formatting | bytes 2048 | tf_op jit(solution)/shard_map/broadcast_in_dim;squeeze | solution.py:547
  7.5 1.0 bitcast_convert_fusion.1
  8.4 0.7 pad_maximum_fusion.own_ref
  9.1 85.0 %shard_map.136 = (bf16[256,4096]{1,0:T(8,128)(2,1)}, bf16[256,4096]{1,0:T(8,128)(2,1)}, f32[256,256]{1,0:T(8,128)}, f32[32,256]{1,0:T(8,128)}, f32[8,128]{1,0:T(8,128)}) custom-call(s32[1]{0:T(128)S(6)} %select_n.7.bit_ref, bf16[288,256]{1,0:T(8,128)(2,1)} %pad_maximum_fusion.own_ref, f32[256,256]{1,0:T(8,128)} %bitcast.24, f32[32,256]{1,0:T(8,128)} %bitcast.26, ...), custom_call_target="tpu_custom_call" | custom-call | tf_op jit(solution)/shard_map/pallas_call | solution.py:487
  94.2 1.3 %fusion = (f32[1,32]{1,0:T(1,128)}, f32[1,32]{1,0:T(1,128)}) fusion(f32[8,128]{1,0:T(8,128)} %get-tuple-element.15), kind=kLoop, calls=%fused_computation.4 | loop fusion | bytes 512 | tf_op jit(solution)/shard_map/slice | solution.py:560
  95.5 0.0 copy-start
  95.5 3.3 %copy.25 = bf16[1,1,256,4096]{3,2,1,0:T(8,128)(2,1)} copy(bf16[1,1,256,4096]{3,2,1,0:T(8,128)(2,1)} %bitcast.23) | data formatting | bytes 4194304
  98.8 0.0 copy-done
  98.8 0.0 copy-start.1
  98.8 0.0 copy-start.2
  98.8 1.3 %copy.26 = bf16[1,1,256,4096]{3,2,1,0:T(8,128)(2,1)} copy(bf16[1,1,256,4096]{3,2,1,0:T(8,128)(2,1)S(1)} %bitcast.22) | data formatting | bytes 4194304
  100.1 0.0 copy-done.1
  100.1 0.7 copy.27
  100.8 0.0 copy-done.2
  100.8 0.6 copy.28
  (1 shorter events, 0.0 us)
Async XLA Ops:
  95.5 3.3 %copy-start = (bf16[256,4096]{1,0:T(8,128)(2,1)S(1)}, bf16[256,4096]{1,0:T(8,128)(2,1)}, u32[]{:S(2)}) copy-start(bf16[256,4096]{1,0:T(8,128)(2,1)} %get-tuple-element.12) | copy-start | bytes 6291460
  98.8 1.3 %copy-start.1 = (f32[256,256]{1,0:T(8,128)S(1)}, f32[256,256]{1,0:T(8,128)}, u32[]{:S(2)}) copy-start(f32[256,256]{1,0:T(8,128)} %get-tuple-element.13) | copy-start | bytes 786436
  98.8 2.0 %copy-start.2 = (f32[32,256]{1,0:T(8,128)S(1)}, f32[32,256]{1,0:T(8,128)}, u32[]{:S(2)}) copy-start(f32[32,256]{1,0:T(8,128)} %get-tuple-element.14) | copy-start | bytes 98308
where the time goes:
time: 102 us; the launch traced here: 101 us
  Pallas kernels  85 us (83%)
  local copies, waits for them, and re-layouts  11.4 us (11%)
  other arithmetic  3.66 us (4%)
  between operations  1.32 us (1%)
    pallas_call x1, Pallas kernels, on_device(): pl.pallas_call(functools.partial(layer_kernel, (heads, reps, seqs, chunk,...  85 us
    unnamed x10, local copies, waits for them, and re-layouts  5.93 us

commit v1 on v0

v1 whole, which is shorter than its diff:
```python
import functools

import jax
import jax.numpy as jnp
from jax import lax
from jax.experimental import pallas as pl
from jax.experimental.pallas import tpu as pltpu
from jax.sharding import PartitionSpec as P

MESH = pl.DeviceIdType.MESH
F32 = jnp.float32
BF16 = jnp.bfloat16
HIGH = lax.Precision.HIGHEST
LOG2E = 1.4426950408889634
TINY = 1e-37
CAP = 60.0
RATE = 0.1
EPS = 1e-6
WIDTH = 128
UNROLL = 2
BARRIER_NEAR = True


def nn(a, b, precision=None):
    return lax.dot_general(
        a, b, (((1,), (0,)), ((), ())), precision=precision, preferred_element_type=F32
    )


def nt(a, b, precision=None):
    return lax.dot_general(
        a, b, (((1,), (1,)), ((), ())), precision=precision, preferred_element_type=F32
    )


def split3(value):
    high = value.astype(BF16).astype(F32)
    rest = value - high
    mid = rest.astype(BF16).astype(F32)
    return high, mid, rest - mid


def split2(value):
    high = value.astype(BF16)
    return high, (value - high.astype(F32)).astype(BF16)


def triple(product, a, b):
    ah, al = split2(a)
    bh, bl = split2(b)
    return product(ah, bh) + (product(ah, bl) + product(al, bh))


def exact(product, parts, b):
    high, mid, low = (part.astype(BF16) for part in parts)
    return product(high, b) + (product(mid, b) + product(low, b))


def layer_kernel(
    dims,
    state_ref,
    step_ref,
    ep_ref,
    decay_ref,
    bias_ref,
    hid_hbm,
    val_hbm,
    cot_hbm,
    lay_hbm,
    sgr_hbm,
    nstate_ref,
    nstep_ref,
    ndecay_ref,
    nbias_ref,
    hid,
    val,
    cot,
    wts,
    gmat,
    dwo,
    acc,
    from_core,
    hop1,
    hop2,
    from_z,
    part_p,
    part_g,
    part_s,
    zsend,
    gsend,
    zero_sum,
    keep,
    heads_in,
    sums_in,
    final_send,
    head_own_s,
    lay,
    sgr,
    feat,
    logit_s,
    mask_s,
    du3,
    rhs,
    scores,
    ds0,
    ds1,
    mrow,
    mcol,
    fgt,
    fg,
    fgl,
    local_sem,
    ssem,
    rsem,
):
    heads, seqs, chunk, rows, bit = dims
    half = rows // 2
    state2 = 2 * WIDTH
    me = lax.axis_index("fsdp")
    rep = lax.axis_index("rep")
    core = lax.rem(me, 2)
    x_at = lax.rem(lax.div(me, 2), 4)
    z_at = lax.div(me, 8)

    def index_of(z, x, c):
        return z * 8 + lax.rem(x, 4) * 2 + c

    other_z = 1 - z_at
    other_c = 1 - core
    right = {"fsdp": index_of(z_at, x_at + 1, core)}
    left = {"fsdp": index_of(z_at, x_at + 3, core)}
    across = {"fsdp": index_of(other_z, x_at, core)}
    twin = {"fsdp": index_of(z_at, x_at, other_c)}
    peers = [{"fsdp": lax.rem(me + k, seqs)} for k in range(1, seqs)]
    gap = 1 << bit
    mate = {"rep": rep + gap * (1 - 2 * lax.rem(lax.div(rep, gap), 2))}

    used = [0]
    started = []

    def remote(src, dst, number, device):
        return pltpu.make_async_remote_copy(
            src_ref=src,
            dst_ref=dst,
            send_sem=ssem.at[number],
            recv_sem=rsem.at[number],
            device_id=device,
            device_id_type=MESH,
        )

    def send(src, dst, device):
        number = used[0]
        used[0] += 1
        copy = remote(src, dst, number, device)
        copy.start()
        started.append(copy)
        return number

    def landed(dst, number):
        remote(dst, dst, number, twin).wait_recv()

    barrier = pltpu.get_barrier_semaphore()
    near = (twin, right, left, across, mate) if BARRIER_NEAR else peers + [mate]
    for device in near:
        pl.semaphore_signal(barrier, inc=1, device_id=device, device_id_type=MESH)
    loads = [
        pltpu.make_async_copy(val_hbm, val, local_sem.at[0]),
        pltpu.make_async_copy(cot_hbm, cot, local_sem.at[1]),
        pltpu.make_async_copy(hid_hbm, hid, local_sem.at[2]),
    ]
    for load in loads:
        load.start()

    wts[me, :state2] = state_ref[...].astype(BF16)
    wts[me, state2:] = step_ref[...].astype(BF16)
    at_u = lax.broadcasted_iota(jnp.int32, (chunk, chunk), 0)
    at_t = lax.broadcasted_iota(jnp.int32, (chunk, chunk), 1)
    ep_t = jnp.broadcast_to(ep_ref[...].astype(F32), (chunk, chunk))
    mask_s[...] = jnp.where((at_u <= at_t) & (ep_t.T == ep_t), 1.0, 0.0)
    eye_r = lax.broadcasted_iota(jnp.int32, (heads, heads), 0)
    eye_c = lax.broadcasted_iota(jnp.int32, (heads, heads), 1)

    def column(row_ref):
        spread_row = jnp.broadcast_to(row_ref[...], (heads, heads))
        return jnp.sum(jnp.where(eye_r == eye_c, spread_row, 0.0), axis=1, keepdims=True)

    decay = -jnp.exp(column(decay_ref))
    bias_col = column(bias_ref)
    place_r = lax.broadcasted_iota(jnp.int32, (heads, WIDTH), 0)
    place_c = lax.broadcasted_iota(jnp.int32, (heads, WIDTH), 1)
    place_d = jnp.where(place_c == place_r, 1.0, 0.0)
    place_b = jnp.where(place_c == place_r + heads, 1.0, 0.0)
    head_own_s[...] = nn(jnp.broadcast_to(decay_ref[...], (8, heads)), place_d, HIGH) + nn(
        jnp.broadcast_to(bias_ref[...], (8, heads)), place_b, HIGH
    )
    feat[...] = jnp.zeros_like(feat)
    logit_s[...] = jnp.zeros_like(logit_s)
    ds0[...] = jnp.zeros_like(ds0)
    ds1[...] = jnp.zeros_like(ds1)
    pl.semaphore_wait(barrier, len(near))

    top = pl.ds(0, half)
    low = pl.ds(half, half)
    halves = (top, low)

    def pass_on(index, part, device):
        return send(wts.at[index, part], wts.at[index, part], device)

    n_across = [pass_on(me, part, across) for part in halves]
    n_rt = pass_on(me, top, right)
    n_ll = pass_on(me, low, left)
    n_rl = pass_on(me, low, right)
    n_lt = pass_on(me, top, left)

    def share(index):
        return send(wts.at[index], wts.at[index], twin)

    n_own = share(me)

    row_id = lax.broadcasted_iota(jnp.int32, (WIDTH, chunk), 0)
    loads[0].wait()
    loads[1].wait()

    def prepare(pair, carry):
        for k in range(2):
            h = pair * 2 + k
            lane = ((row_id & (heads - 1)) == h) & (row_id < 3 * heads)
            rhs[h] = jnp.where(lane, 1.0, 0.0).astype(BF16)
            lanes = pl.ds(pl.multiple_of(h * WIDTH, WIDTH), WIDTH)
            xh = val[:, lanes]
            gh = cot[:, lanes]
            gmat[h, :WIDTH] = nt(xh[:WIDTH], gh)
            gmat[h, WIDTH:, WIDTH:] = nt(xh[WIDTH:], gh[WIDTH:])
        return carry

    lax.fori_loop(0, heads // 2, prepare, 0)
    loads[2].wait()

    def columns(index):
        return pl.ds(pl.multiple_of(index * chunk, chunk), chunk)

    def feat_part(index):
        tokens = hid[:, columns(index)]
        feat[...] += nn(tokens, wts[index, :state2, :])
        logit_s[:, :heads] += nt(tokens, wts[index, state2:, :])

    def spread(z, n_rt, n_rl, n_ll, n_lt):
        at_l = index_of(z, x_at + 3, core)
        at_r = index_of(z, x_at + 1, core)
        landed(wts.at[at_l, top], n_rt)
        f_r = pass_on(at_l, top, right)
        landed(wts.at[at_r, low], n_ll)
        f_l = pass_on(at_r, low, left)
        landed(wts.at[at_l, low], n_rl)
        t_l = share(at_l)
        landed(wts.at[at_r, top], n_lt)
        t_r = share(at_r)
        return at_l, at_r, f_r, f_l, t_l, t_r

    def shared(z, dx, number):
        index = index_of(z, x_at + dx, other_c)
        landed(wts.at[index], number)
        feat_part(index)

    at_l, at_r, f_r, f_l, t_l, t_r = spread(z_at, n_rt, n_rl, n_ll, n_lt)
    feat_part(me)
    shared(z_at, 0, n_own)
    at_z = index_of(other_z, x_at, core)
    landed(wts.at[at_z, top], n_across[0])
    z_rt = pass_on(at_z, top, right)
    feat_part(at_l)
    landed(wts.at[at_z, low], n_across[1])
    z_ll = pass_on(at_z, low, left)
    z_rl = pass_on(at_z, low, right)
    z_lt = pass_on(at_z, top, left)
    t_z = share(at_z)
    at_2 = index_of(z_at, x_at + 2, core)
    landed(wts.at[at_2, top], f_r)
    landed(wts.at[at_2, low], f_l)
    t_2 = share(at_2)
    feat_part(at_r)
    feat_part(at_z)
    feat_part(at_2)
    shared(z_at, 3, t_l)
    shared(z_at, 1, t_r)
    shared(other_z, 0, t_z)
    shared(z_at, 2, t_2)
    at_l, at_r, f_r, f_l, t_l, t_r = spread(other_z, z_rt, z_rl, z_ll, z_lt)
    feat_part(at_l)
    feat_part(at_r)
    shared(other_z, 3, t_l)
    shared(other_z, 1, t_r)
    at_2 = index_of(other_z, x_at + 2, core)
    landed(wts.at[at_2, top], f_r)
    t_2t = pass_on(at_2, top, twin)
    landed(wts.at[at_2, low], f_l)
    t_2l = pass_on(at_2, low, twin)
    feat_part(at_2)
    at_2 = index_of(other_z, x_at + 2, other_c)
    landed(wts.at[at_2, top], t_2t)
    landed(wts.at[at_2, low], t_2l)
    feat_part(at_2)

    n_part_p = send(wts.at[me], part_p, mate)

    logits = logit_s[...].T[:heads] + bias_col
    small = jnp.exp(-jnp.abs(logits))
    log_part = jnp.where(
        small < 0.01, small * (1.0 - small * (0.5 - small * (1.0 / 3.0))), jnp.log(1.0 + small)
    )
    step = jnp.maximum(logits, 0.0) + log_part
    gate = jnp.where(logits >= 0.0, 1.0, small) / (1.0 + small)
    step_safe = jnp.maximum(step, TINY)
    ratio = jnp.where(logits < -20.0, 1.0, gate / step_safe)
    upper = jnp.where(at_u <= at_t, 1.0, 0.0).astype(BF16)
    c2 = exact(nn, split3(decay * step), upper) * LOG2E
    du = jnp.log2(step_safe) - c2
    parts = split3(du) + (jnp.ones((WIDTH - 3 * heads, chunk), F32),)
    du3[...] = jnp.concatenate(parts, axis=0).T.astype(BF16)
    c_parts = split3(c2)
    for k in range(3):
        rhs[:, 3 * heads + k, :] = c_parts[k].astype(BF16)
    b_proj = feat[:, :WIDTH]
    c_proj = feat[:, WIDTH:]
    scores[...] = jnp.where(mask_s[...] > 0.5, triple(nt, b_proj, c_proj), 0.0)
    ones8 = jnp.ones((8, WIDTH), BF16)

    def head_group(group, carry):
        p0 = 0.0
        p1 = 0.0
        for k in range(UNROLL):
            h = group * UNROLL + k
            lanes = pl.ds(pl.multiple_of(h * WIDTH, WIDTH), WIDTH)
            gh = cot[:, lanes]
            rh = rhs[h]
            g0 = gmat[h, :WIDTH]
            g1 = gmat[h, WIDTH:, WIDTH:]
            e0 = jnp.exp2(jnp.minimum(nn(du3[:WIDTH], rh), CAP))
            e1 = jnp.exp2(jnp.minimum(nn(du3[WIDTH:], rh[:, WIDTH:]), CAP))
            p0 = p0 + g0 * e0
            p1 = p1 + g1 * e1
            v0 = e0 * scores[:WIDTH]
            v1 = e1 * scores[WIDTH:, WIDTH:]
            v0 = v0.astype(BF16)
            v1 = v1.astype(BF16)
            m0 = jnp.sum((v0.astype(F32) * g0).reshape(WIDTH // 8, 8, -1), axis=0)
            m1 = jnp.sum((v1.astype(F32) * g1).reshape(WIDTH // 8, 8, -1), axis=0)
            mrow[h, :, :WIDTH] = m0[:, :WIDTH]
            mrow[h, :, WIDTH:] = m0[:, WIDTH:] + m1
            dx0 = nn(v0, gh)
            dx1 = nn(v1, gh[WIDTH:])
            dx = jnp.concatenate([dx0, dx1], axis=0)
            sgr[:, lanes] = dx.astype(BF16)
            high, rest = split2(dx * val[:, lanes].astype(F32))
            mcol[h] = nt(ones8, high) + nt(ones8, rest)
        ds0[...] += p0
        ds1[...] += p1
        return carry

    lax.fori_loop(0, heads // UNROLL, head_group, 0)
    out_sgr = pltpu.make_async_copy(sgr, sgr_hbm, local_sem.at[4])
    out_sgr.start()

    lower = jnp.where(at_u >= at_t, 1.0, 0.0).astype(BF16)
    mc = jnp.sum(mcol[...], axis=1) * 0.125
    drate = exact(nn, split3(jnp.sum(mrow[...], axis=1) - mc), lower)
    dlogit = mc * ratio + gate * (decay * drate)
    ddecay = decay * step * drate
    stack = jnp.concatenate(
        [ddecay, dlogit, jnp.zeros((WIDTH - 2 * heads, chunk), F32)], axis=0
    )
    ds_full = jnp.concatenate(
        [
            ds0[...],
            jnp.concatenate([jnp.zeros((WIDTH, WIDTH), F32), ds1[...]], axis=1),
        ],
        axis=0,
    )
    ds_full = jnp.where(mask_s[...] > 0.5, ds_full, 0.0)
    db = triple(nn, ds_full, c_proj)
    dct = triple(nn, b_proj.T, ds_full)
    fgt[:WIDTH] = db.T.astype(BF16)
    fgt[WIDTH:state2] = dct.astype(BF16)
    fgt[state2:] = dlogit.astype(BF16)

    places = [(z, dx) for z in (other_z, z_at) for dx in (2, 1, 3, 0)]
    n_core = {}

    def twin_part(slot):
        z, dx = places[slot]
        index = index_of(z, x_at + dx, other_c)
        dwo[slot] = nn(fgt[...], hid[:, columns(index)]).astype(BF16)
        n_core[slot] = send(dwo.at[slot], from_core.at[slot], twin)

    def own_part(slot):
        z, dx = places[slot]
        index = index_of(z, x_at + dx, core)
        total = nn(fgt[...], hid[:, columns(index)])
        landed(from_core.at[slot], n_core[slot])
        return total + from_core[slot].astype(F32)

    def layer_part(index):
        spot = columns(index)
        w = wts[index]
        lay[:, spot] = (
            nt(fg[...], w[:state2]) + nn(fgl[:, :heads], w[state2:])
        ).astype(BF16)

    def ring_first(base, k):
        twin_part(base)
        twin_part(base + 1)
        acc[base] = own_part(base).astype(BF16)
        r1 = send(acc.at[base, top], hop1.at[k, 0], right)
        l1 = send(acc.at[base, low], hop1.at[k, 1], left)
        twin_part(base + 2)
        plus = own_part(base + 1)
        acc[base + 1, low] = plus[half:].astype(BF16)
        keep[k, 0] = plus[:half]
        r2 = send(acc.at[base + 1, low], hop2.at[k, 0, low], right)
        twin_part(base + 3)
        minus = own_part(base + 2)
        acc[base + 2, top] = minus[:half].astype(BF16)
        keep[k, 1] = minus[half:]
        l2 = send(acc.at[base + 2, top], hop2.at[k, 1, top], left)
        return r1, l1, r2, l2

    def ring_next(base, k, r1, l1):
        landed(hop1.at[k, 0], r1)
        acc[base + 1, top] = (keep[k, 0] + hop1[k, 0].astype(F32)).astype(BF16)
        r3 = send(acc.at[base + 1, top], hop2.at[k, 0, top], right)
        landed(hop1.at[k, 1], l1)
        acc[base + 2, low] = (keep[k, 1] + hop1[k, 1].astype(F32)).astype(BF16)
        l3 = send(acc.at[base + 2, low], hop2.at[k, 1, low], left)
        zero_sum[k] = own_part(base + 3)
        return r3, l3

    def ring_end(k, part, first, second):
        landed(hop2.at[k, 0, part], first)
        landed(hop2.at[k, 1, part], second)
        return (
            zero_sum[k, part, :]
            + hop2[k, 0, part, :].astype(F32)
            + hop2[k, 1, part, :].astype(F32)
        )

    r1, l1, r2, l2 = ring_first(0, 0)
    r3, l3 = ring_next(0, 0, r1, l1)
    s1, m1, s2, m2 = ring_first(4, 1)
    zsend[top, :] = ring_end(0, top, r3, l2).astype(BF16)
    n_z = [send(zsend.at[top], from_z.at[top], across)]
    zsend[low, :] = ring_end(0, low, r2, l3).astype(BF16)
    n_z.append(send(zsend.at[low], from_z.at[low], across))
    s3, m3 = ring_next(4, 1, s1, m1)

    sums8 = exact(lambda a, b: nt(b, a), split3(stack), jnp.ones((8, chunk), BF16))
    heads_in[me] = sums8
    n_heads = [send(heads_in.at[me], heads_in.at[me], device) for device in peers]
    fg[:, :WIDTH] = db.astype(BF16)
    fg[:, WIDTH:] = dct.T.astype(BF16)
    wide = jnp.concatenate([dlogit, jnp.zeros((WIDTH - heads, chunk), F32)], axis=0)
    fgl[...] = wide.T.astype(BF16)
    for index in range(seqs):
        layer_part(index)
    out_lay = pltpu.make_async_copy(lay, lay_hbm, local_sem.at[5])
    out_lay.start()

    for k, number in enumerate(n_heads):
        landed(heads_in.at[lax.rem(me + seqs - k - 1, seqs)], number)
    head_grad = jnp.sum(heads_in[...], axis=0)[:1]
    head_own = head_own_s[:1]
    head_sq = jnp.sum(head_own * head_own, axis=1, keepdims=True) / (2 * heads)
    hgrad_sq = jnp.sum(head_grad * head_grad, axis=1, keepdims=True) / (2 * heads)
    head_trust = jnp.sqrt(head_sq) / jnp.sqrt(hgrad_sq + EPS)
    final_send[:1] = head_own - RATE * head_trust * head_grad

    def lanes_sum(value):
        total = jnp.sum(value * value, axis=0, keepdims=True)
        return total[:, :WIDTH] + total[:, WIDTH:]

    state_own = state_ref[...]
    step_own = step_ref[...]
    own_sq = [lanes_sum(state_own), lanes_sum(step_own)]

    total_t = ring_end(1, top, s3, m2)
    total_l = ring_end(1, low, s2, m3)
    landed(from_z.at[top], n_z[0])
    grad_t = total_t + from_z[top, :].astype(F32)
    gsend[top, :] = grad_t.astype(BF16)
    n_part_g = [send(gsend.at[top], part_g.at[top], mate)]
    landed(from_z.at[low], n_z[1])
    grad_l = total_l + from_z[low, :].astype(F32)
    gsend[low, :] = grad_l.astype(BF16)
    n_part_g.append(send(gsend.at[low], part_g.at[low], mate))
    grad = jnp.concatenate([grad_t, grad_l], axis=0)

    sums_in[me] = jnp.concatenate(
        [lanes_sum(grad[:state2]), lanes_sum(grad[state2:])]
        + own_sq
        + [jnp.zeros((4, WIDTH), F32)],
        axis=0,
    )
    n_sums = [send(sums_in.at[me], sums_in.at[me], device) for device in peers]
    for k, number in enumerate(n_sums):
        landed(sums_in.at[lax.rem(me + seqs - k - 1, seqs)], number)
    squares = jnp.sum(jnp.sum(sums_in[...], axis=0), axis=1, keepdims=True)
    width = seqs * chunk
    state_trust = jnp.sqrt(squares[2:3] / (width * state2)) / jnp.sqrt(
        squares[0:1] / (width * state2) + EPS
    )
    step_trust = jnp.sqrt(squares[3:4] / (width * heads)) / jnp.sqrt(
        squares[1:2] / (width * heads) + EPS
    )
    final_send[1:2] = jnp.broadcast_to(state_trust, (1, WIDTH))
    final_send[2:3] = jnp.broadcast_to(step_trust, (1, WIDTH))
    n_final = send(final_send, part_s, mate)
    landed(part_p, n_part_p)
    landed(part_g.at[top], n_part_g[0])
    landed(part_g.at[low], n_part_g[1])
    mate_p = part_p[...].astype(F32)
    mate_g = part_g[...].astype(F32)
    base_state = 0.5 * (state_own + mate_p[:state2]) - (0.5 * RATE) * (
        state_trust * grad[:state2].T
    )
    base_step = 0.5 * (step_own + mate_p[state2:]) - (0.5 * RATE) * (step_trust * grad[state2:])
    mate_state = (0.5 * RATE) * mate_g[:state2].T
    mate_step = (0.5 * RATE) * mate_g[state2:]
    landed(part_s, n_final)
    mate_s = part_s[...]
    nstate_ref[...] = base_state - mate_s[1:2, :1] * mate_state
    nstep_ref[...] = base_step - mate_s[2:3, :1] * mate_step
    head_mix = 0.5 * (final_send[:1] + mate_s[:1])
    ndecay_ref[...] = head_mix[:, :heads]
    nbias_ref[...] = head_mix[:, heads : 2 * heads]

    out_sgr.wait()
    out_lay.wait()
    for copy in started:
        copy.wait_send()


def place_kernel(*refs):
    count = (len(refs) - 1) // 2
    sem = refs[-1]
    copies = [
        pltpu.make_async_copy(refs[k], refs[count + k], sem.at[k]) for k in range(count)
    ]
    for copy in copies:
        copy.start()
    for copy in copies:
        copy.wait()


def on_device(
    hidden_in, scan_in, grad_out, episodes, gossip_step, state_proj, step_proj, decay_log, step_bias
):
    reps = lax.axis_size("rep")
    seqs = lax.axis_size("fsdp")
    bits = reps.bit_length() - 1
    heads = step_proj.shape[1]
    length, inner = scan_in.shape[2:]
    model = hidden_in.shape[3]
    chunk = model // seqs
    state2 = 2 * WIDTH
    rows = state2 + heads
    half = rows // 2
    vmem = pl.BlockSpec(memory_space=pltpu.VMEM)
    anyspace = pl.BlockSpec(memory_space=pl.ANY)
    copies = 100
    shapes = (
        jax.ShapeDtypeStruct((length, model), BF16),
        jax.ShapeDtypeStruct((length, inner), BF16),
        jax.ShapeDtypeStruct((chunk, state2), F32),
        jax.ShapeDtypeStruct((heads, chunk), F32),
        jax.ShapeDtypeStruct((1, heads), F32),
        jax.ShapeDtypeStruct((1, heads), F32),
    )

    def run(bit, *operands):
        outs = pl.pallas_call(
            functools.partial(layer_kernel, (heads, seqs, chunk, rows, bit)),
            out_shape=shapes,
            in_specs=[vmem] * 5 + [anyspace] * 3,
            out_specs=(anyspace, anyspace, vmem, vmem, vmem, vmem),
            scratch_shapes=[
                pltpu.VMEM((length, model), BF16),
                pltpu.VMEM((length, inner), BF16),
                pltpu.VMEM((length, inner), BF16),
                pltpu.VMEM((seqs, rows, chunk), BF16),
                pltpu.VMEM((heads, length, length), F32),
                pltpu.VMEM((8, rows, chunk), BF16),
                pltpu.VMEM((8, rows, chunk), BF16),
                pltpu.VMEM((8, rows, chunk), BF16),
                pltpu.VMEM((2, 2, half, chunk), BF16),
                pltpu.VMEM((2, 2, rows, chunk), BF16),
                pltpu.VMEM((rows, chunk), BF16),
                pltpu.VMEM((rows, chunk), BF16),
                pltpu.VMEM((rows, chunk), BF16),
                pltpu.VMEM((8, WIDTH), F32),
                pltpu.VMEM((rows, chunk), BF16),
                pltpu.VMEM((rows, chunk), BF16),
                pltpu.VMEM((2, rows, chunk), F32),
                pltpu.VMEM((2, 2, half, chunk), F32),
                pltpu.VMEM((seqs, 8, WIDTH), F32),
                pltpu.VMEM((seqs, 8, WIDTH), F32),
                pltpu.VMEM((8, WIDTH), F32),
                pltpu.VMEM((8, WIDTH), F32),
                pltpu.VMEM((length, model), BF16),
                pltpu.VMEM((length, inner), BF16),
                pltpu.VMEM((length, state2), F32),
                pltpu.VMEM((length, WIDTH), F32),
                pltpu.VMEM((length, length), F32),
                pltpu.VMEM((length, WIDTH), BF16),
                pltpu.VMEM((heads, WIDTH, length), BF16),
                pltpu.VMEM((length, length), F32),
                pltpu.VMEM((WIDTH, length), F32),
                pltpu.VMEM((WIDTH, WIDTH), F32),
                pltpu.VMEM((heads, 8, length), F32),
                pltpu.VMEM((heads, 8, length), F32),
                pltpu.VMEM((rows, length), BF16),
                pltpu.VMEM((length, state2), BF16),
                pltpu.VMEM((length, WIDTH), BF16),
                pltpu.SemaphoreType.DMA((6,)),
                pltpu.SemaphoreType.DMA((copies,)),
                pltpu.SemaphoreType.DMA((copies,)),
            ],
            compiler_params=pltpu.CompilerParams(
                collective_id=bit, has_side_effects=True, vmem_limit_bytes=38 * 1024 * 1024
            ),
        )(*operands)
        return tuple(
            pl.pallas_call(
                place_kernel,
                out_shape=shapes,
                in_specs=[anyspace] * len(shapes),
                out_specs=(anyspace,) * len(shapes),
                scratch_shapes=[pltpu.SemaphoreType.DMA((len(shapes),))],
                compiler_params=pltpu.CompilerParams(vmem_limit_bytes=1024 * 1024),
            )(*outs)
        )

    operands = (
        state_proj[0],
        step_proj[0],
        episodes[0],
        decay_log,
        step_bias,
        hidden_in[0, 0],
        scan_in[0, 0],
        grad_out[0, 0],
    )
    outs = lax.switch(
        lax.rem(gossip_step[0], bits), [functools.partial(run, bit) for bit in range(bits)], *operands
    )
    layer_grad, scan_grad, new_state, new_step, new_decay, new_bias = outs
    return (
        layer_grad[None, None],
        scan_grad[None, None],
        new_state[None],
        new_step[None],
        new_decay,
        new_bias,
    )


def solution(mesh):
    in_specs = (
        P("rep", "fsdp", None, None),
        P("rep", "fsdp", None, None),
        P("rep", "fsdp", None, None),
        P("rep", "fsdp", None),
        P(),
        P("rep", "fsdp", None),
        P("rep", None, "fsdp"),
        P("rep", None),
        P("rep", None),
    )
    out_specs = (
        P("rep", "fsdp", None, None),
        P("rep", "fsdp", None, None),
        P("rep", "fsdp", None),
        P("rep", None, "fsdp"),
        P("rep", None),
        P("rep", None),
    )
    return jax.shard_map(
        on_device, mesh=mesh, in_specs=in_specs, out_specs=out_specs, check_vma=False
    )
```

time: 102 us -> 75 us (0.74)
  the two profiles are of different devices: /device:TPU:1 before, /device:TPU:32 now
where the time goes in v1:
time: 75 us; the launch traced here: 75.7 us
  Pallas kernels  73.4 us (98%)
  between operations  1.51 us (2%)
  loops' own time  0.82 us (1%)
    pallas_call x1, Pallas kernels, run(): pl.pallas_call(functools.partial(layer_kernel, (heads, seqs, chunk, rows,...  71.2 us
    pallas_call x1, Pallas kernels, run(): pl.pallas_call(place_kernel, out_shape=shapes, in_specs=[anyspace] * len(...  2.14 us

profile of v1, /device:TPU:32, one launch (start us, length us, event | category | flops | bytes accessed | tf_op | source)
XLA Modules:
  0.0 75.7 jit_solution(16958019838920374749)
XLA Ops:
  1.3 74.2 %conditional.1 = ((bf16[256,4096]{1,0:T(8,128)(2,1)}, bf16[256,4096]{1,0:T(8,128)(2,1)}, f32[256,256]{1,0:T(8,128)}, f32[32,256]{1,0:T(8,128)}, f32[1,32]{1,0:T(1,128)}, /*index=5*/f32[1,32]{1,0:T(1,128)})) conditional(s32[]{:T(128)} %clamp.3, (f32[256,256]{1,0:T(8,128)}, f32[32,256]{1,0:T(8,128)}, ...), branch_computations={%region_0.0_spmd.clone, %region_1.0_spmd.clone, %region_2.0_spmd.c... | conditional | bytes 8 | solution.py:651
  1.8 71.2 %branch_3_fun.4 = (bf16[256,4096]{1,0:T(8,128)(2,1)S(1)}, bf16[256,4096]{1,0:T(8,128)(2,1)S(1)}, f32[256,256]{1,0:T(8,128)S(1)}, f32[32,256]{1,0:T(8,128)S(1)}, ...) custom-call(f32[256,256]{1,0:T(8,128)} %get-tuple-element.259.state_ref, f32[32,256]{1,0:T(8,128)} %get-tuple-element.260.step_ref, ...), custom_call_target="tpu_custom_call" | custom-call | tf_op jit(solution)/shard_map/cond/branch_3_fun/pallas_call | solution.py:579
  73.0 2.1 %branch_3_fun.5 = (bf16[256,4096]{1,0:T(8,128)(2,1)}, bf16[256,4096]{1,0:T(8,128)(2,1)}, f32[256,256]{1,0:T(8,128)}, f32[32,256]{1,0:T(8,128)}, f32[1,32]{1,0:T(1,128)}, /*index=5*/f32[1,32]{1,0:T(1,128)}) custom-call(bf16[256,4096]{1,0:T(8,128)(2,1)S(1)} %get-tuple-element.267.refs_0_, bf16[256,4096]{1,0:T(8,128)(2,1)S(1)} %get-tuple-element.268.refs_1_, ...), custom_call_target="tpu_custom_call" | custom-call | tf_op jit(solution)/shard_map/cond/branch_3_fun/pallas_call | solution.py:631
